TPU v7x, 256 devices: a whole 4x4x8 slice. The times are simulated.
256 devices in a mesh: section: 128 (over z, y, x), attn: 2 (over core).
Axes of the slice: x: 4, y: 4, z: 8, core: 2. Of those that a mesh axis runs over, the one named last changes fastest.
Arguments:
- queries: bfloat16 [65536, 3072], P(('section', 'attn')), may hold values from -120 to 120
- keys: bfloat16 [65536, 1024], P(('section', 'attn')), may hold values from -2.5 to 2.5
- values: bfloat16 [65536, 1024], P(('section', 'attn')), may hold values from -4 to 4
- doc_ids: int32 [65536], replicated, may hold values from 0 to 127, never falling along the last dimension, each value on 1 to 1792 neighbouring positions
Outputs:
- attended: bfloat16 [65536, 3072], P(('section', 'attn'))
Inputs may be any that keep to these rules, and one draw needn't show every extreme that they name: `doc_ids`: along the pack the document numbers never fall, and a document holds at most 1792 tokens.
All inputs are finite; a program needn't handle non-finite values.
Results may differ from a plain program's by a relative error of at most 0.0028.
Values may be sent and summed in bfloat16 or wider, within the bound.
A program may use at most 64 MiB of HBM per device.

v0:
```python
import jax
import jax.numpy as jnp
from jax import lax
from jax.sharding import PartitionSpec as P

KV_HEADS = 8
HEAD_DIM = 128
GROUP = 3
REACH = 8


def passed_along(block, axis, distance):
    devices = range(lax.axis_size(axis))
    route = [(i - distance, i) for i in devices if i - distance in devices]
    return lax.ppermute(block, axis, route)


def fold_piece(carry, query_rows, key_rows, value_rows, query_pos, query_doc, key_pos, key_doc):
    row_max, total, weighted = carry
    head_size = query_rows.shape[-1]
    kv_count = query_rows.shape[1]
    key_heads = key_rows.reshape(key_rows.shape[0], kv_count, head_size)
    value_heads = value_rows.reshape(value_rows.shape[0], kv_count, head_size)
    scores = jnp.einsum(
        "qgrd,kgd->grqk", query_rows, key_heads, preferred_element_type=jnp.float32
    ) * head_size ** (-0.5)
    allowed = (key_pos[None, :] <= query_pos[:, None]) & (key_doc[None, :] == query_doc[:, None])
    scores = jnp.where(allowed, scores, -1e30)
    new_max = jnp.maximum(row_max, jnp.max(scores, axis=-1))
    rescale = jnp.exp(row_max - new_max)
    weights = jnp.exp(scores - new_max[..., None])
    total = total * rescale + jnp.sum(weights, axis=-1)
    product = jnp.einsum(
        "grqk,kgd->grqd",
        weights.astype(jnp.bfloat16),
        value_heads,
        preferred_element_type=jnp.float32,
    )
    weighted = weighted * rescale[..., None] + product
    return (new_max, total, weighted)


def fold_remote(carry, context, key_rows, value_rows, source):
    query_rows, doc_ids, owner = context
    rows = query_rows.shape[0]
    first = source * rows
    key_doc = lax.dynamic_slice_in_dim(doc_ids, jnp.maximum(first, 0), rows)
    query_doc = lax.dynamic_slice_in_dim(doc_ids, owner * rows, rows)
    needed = (source >= 0) & (source < owner) & (key_doc[rows - 1] == query_doc[0])
    key_pos = first + jnp.arange(rows, dtype=jnp.int32)
    query_pos = owner * rows + jnp.arange(rows, dtype=jnp.int32)

    def attend_piece(inner):
        return fold_piece(
            inner, query_rows, key_rows, value_rows, query_pos, query_doc, key_pos, key_doc
        )

    def skip_piece(inner):
        return inner

    return lax.cond(needed, attend_piece, skip_piece, carry)


def fold_window(carry, context, window_keys, window_values, first_source):
    rows = context[0].shape[0]
    pieces = window_keys.shape[0] // rows

    def one_piece(piece_num, inner):
        key_rows = lax.dynamic_slice_in_dim(window_keys, piece_num * rows, rows, 0)
        value_rows = lax.dynamic_slice_in_dim(window_values, piece_num * rows, rows, 0)
        return fold_remote(inner, context, key_rows, value_rows, first_source + piece_num)

    return lax.fori_loop(0, pieces, one_piece, carry)


def shards(queries, keys, values, doc_ids):
    rows = queries.shape[0]
    query_rows = queries.reshape(rows, KV_HEADS, GROUP, HEAD_DIM)
    cores = lax.axis_size("attn")
    chip = lax.axis_index("section")
    owner = chip * cores + lax.axis_index("attn")
    context = (query_rows, doc_ids, owner)
    query_doc = lax.dynamic_slice_in_dim(doc_ids, owner * rows, rows)
    query_pos = owner * rows + jnp.arange(rows, dtype=jnp.int32)
    stat_shape = (KV_HEADS, GROUP, rows)
    carry = (
        jnp.full(stat_shape, -1e30, jnp.float32),
        jnp.zeros(stat_shape, jnp.float32),
        jnp.zeros(stat_shape + (HEAD_DIM,), jnp.float32),
    )
    carry = fold_piece(carry, query_rows, keys, values, query_pos, query_doc, query_pos, query_doc)
    window = (
        lax.all_gather(keys, "attn", axis=0, tiled=True),
        lax.all_gather(values, "attn", axis=0, tiled=True),
    )
    carry = fold_window(carry, context, window[0], window[1], chip * cores)
    hops = (REACH + cores - 2) // cores
    for hop in range(1, hops + 1):
        window = passed_along((window[0], window[1]), "section", 1)
        carry = fold_window(carry, context, window[0], window[1], (chip - hop) * cores)
    row_max, total, weighted = carry
    result = (weighted / total[..., None]).astype(jnp.bfloat16)
    return result.transpose(2, 0, 1, 3).reshape(rows, -1)


def solution(mesh):
    placed = (
        P(("section", "attn"), None),
        P(("section", "attn"), None),
        P(("section", "attn"), None),
        P(),
    )
    return jax.shard_map(
        shards, mesh=mesh, in_specs=placed, out_specs=P(("section", "attn"), None), check_vma=False
    )
```

profile of v0, /device:TPU:46, one launch (start us, length us, event | category | flops | bytes accessed | tf_op | source)
XLA Modules:
  0.0 283.8 jit_solution(12785599930436756468)
XLA Ops:
  10.7 15.0 %all-gather.3.cloned.1.call-done = bf16[512,1024]{0,1:T(8,128)(2,1)} async-done(((bf16[256,1024]{0,1:T(8,128)(2,1)}), bf16[512,1024]{0,1:T(8,128)(2,1)}) %all-gather.3.cloned.1.call-update) | async-done | bytes 1048592 | tf_op jit(solution)/shard_map/all_gather | solution.py:93
  29.1 13.9 %all-gather.5.cloned.1.call-done = bf16[512,1024]{0,1:T(8,128)(2,1)} async-done(((bf16[256,1024]{0,1:T(8,128)(2,1)}), bf16[512,1024]{0,1:T(8,128)(2,1)}) %all-gather.5.cloned.1.call-update) | async-done | bytes 1048592 | tf_op jit(solution)/shard_map/all_gather | solution.py:94
  46.4 7.5 %collective-permute-done = bf16[512,1024]{0,1:T(8,128)(2,1)S(1)} collective-permute-done((bf16[512,1024]{0,1:T(8,128)(2,1)}, bf16[512,1024]{0,1:T(8,128)(2,1)S(1)}, u32[]{:S(2)}, u32[]{:S(2)}) %collective-permute-start) | collective-permute-done | bytes 1048608 | tf_op jit(solution)/shard_map/ppermute | solution.py:15
  59.4 17.0 %collective-permute-done.1 = bf16[512,1024]{0,1:T(8,128)(2,1)S(1)} collective-permute-done((bf16[512,1024]{0,1:T(8,128)(2,1)}, bf16[512,1024]{0,1:T(8,128)(2,1)S(1)}, u32[]{:S(2)}, u32[]{:S(2)}) %collective-permute-start.1) | collective-permute-done | bytes 1048608 | tf_op jit(solution)/shard_map/ppermute | solution.py:15
  76.3 5.5 %collective-permute-start.3 = (bf16[512,1024]{0,1:T(8,128)(2,1)S(1)}, bf16[512,1024]{0,1:T(8,128)(2,1)}, u32[]{:S(2)}, u32[]{:S(2)}) collective-permute-start(bf16[512,1024]{0,1:T(8,128)(2,1)S(1)} %collective-permute-done.1), channel_id=1, source_target_pairs={{0,2},{2,4},{4,6},{6,8},{8,10},{10,12},{12,14},{14,16},{16,18},{18... | collective-permute-start | bytes 3145736 | tf_op jit(solution)/shard_map/ppermute | solution.py:15
  81.8 17.0 %collective-permute-done.2 = bf16[512,1024]{0,1:T(8,128)(2,1)S(1)} collective-permute-done((bf16[512,1024]{0,1:T(8,128)(2,1)S(1)}, bf16[512,1024]{0,1:T(8,128)(2,1)S(1)}, u32[]{:S(2)}, u32[]{:S(2)}) %collective-permute-start.2) | collective-permute-done | bytes 1048608 | tf_op jit(solution)/shard_map/ppermute | solution.py:15
  98.8 5.5 %collective-permute-start.4 = (bf16[512,1024]{0,1:T(8,128)(2,1)S(1)}, bf16[512,1024]{0,1:T(8,128)(2,1)}, u32[]{:S(2)}, u32[]{:S(2)}) collective-permute-start(bf16[512,1024]{0,1:T(8,128)(2,1)S(1)} %collective-permute-done.2), channel_id=1, source_target_pairs={{0,2},{2,4},{4,6},{6,8},{8,10},{10,12},{12,14},{14,16},{16,18},{18... | collective-permute-start | bytes 3145736 | tf_op jit(solution)/shard_map/ppermute | solution.py:15
  104.3 17.1 %collective-permute-done.3 = bf16[512,1024]{0,1:T(8,128)(2,1)} collective-permute-done((bf16[512,1024]{0,1:T(8,128)(2,1)S(1)}, bf16[512,1024]{0,1:T(8,128)(2,1)}, u32[]{:S(2)}, u32[]{:S(2)}) %collective-permute-start.3) | collective-permute-done | bytes 1048608 | tf_op jit(solution)/shard_map/ppermute | solution.py:15
  121.4 5.5 %collective-permute-start.5 = (bf16[512,1024]{0,1:T(8,128)(2,1)}, bf16[512,1024]{0,1:T(8,128)(2,1)}, u32[]{:S(2)}, u32[]{:S(2)}) collective-permute-start(bf16[512,1024]{0,1:T(8,128)(2,1)} %collective-permute-done.3), channel_id=1, source_target_pairs={{0,2},{2,4},{4,6},{6,8},{8,10},{10,12},{12,14},{14,16},{16,18},{18... | collective-permute-start | bytes 3145736 | tf_op jit(solution)/shard_map/ppermute | solution.py:15
  131.9 11.9 %collective-permute-done.4 = bf16[512,1024]{0,1:T(8,128)(2,1)} collective-permute-done((bf16[512,1024]{0,1:T(8,128)(2,1)S(1)}, bf16[512,1024]{0,1:T(8,128)(2,1)}, u32[]{:S(2)}, u32[]{:S(2)}) %collective-permute-start.4) | collective-permute-done | bytes 1048608 | tf_op jit(solution)/shard_map/ppermute | solution.py:15
  149.3 17.0 %collective-permute-done.5 = bf16[512,1024]{0,1:T(8,128)(2,1)} collective-permute-done((bf16[512,1024]{0,1:T(8,128)(2,1)}, bf16[512,1024]{0,1:T(8,128)(2,1)}, u32[]{:S(2)}, u32[]{:S(2)}) %collective-permute-start.5) | collective-permute-done | bytes 1048608 | tf_op jit(solution)/shard_map/ppermute | solution.py:15
  166.3 5.7 %collective-permute-start.7 = (bf16[512,1024]{0,1:T(8,128)(2,1)}, bf16[512,1024]{0,1:T(8,128)(2,1)}, u32[]{:S(2)}, u32[]{:S(2)}) collective-permute-start(bf16[512,1024]{0,1:T(8,128)(2,1)} %collective-permute-done.5), channel_id=1, source_target_pairs={{0,2},{2,4},{4,6},{6,8},{8,10},{10,12},{12,14},{14,16},{16,18},{18... | collective-permute-start | bytes 3145736 | tf_op jit(solution)/shard_map/ppermute | solution.py:15
  181.1 7.0 %while.95 = (s32[]{:T(128)}, f32[8,3,256]{2,1,0:T(4,128)S(1)}, f32[8,3,256]{2,1,0:T(4,128)S(1)}, f32[8,3,256,128]{3,2,1,0:T(8,128)S(1)}, s32[]{:T(128)}, /*index...) while((s32[]{:T(128)}, f32[8,3,256]{2,1,0:T(4,128)S(1)}, ...), condition=%wide.region_7.8_spmd, body=%wide.region_2.7_spmd.sunk | while | flops 824390144 | bytes 30551492 | solution.py:73
  188.0 22.5 %while.96 = (s32[]{:T(128)}, f32[8,3,256]{2,1,0:T(4,128)S(1)}, f32[8,3,256]{2,1,0:T(4,128)S(1)}, f32[8,3,256,128]{3,2,1,0:T(8,128)S(1)}, s32[]{:T(128)}, /*index...) while((s32[]{:T(128)}, f32[8,3,256]{2,1,0:T(4,128)S(1)}, ...), condition=%wide.region_13.14_spmd, body=%wide.region_8.13_spmd.sunk | while | flops 824390144 | bytes 30551492 | solution.py:73
  191.2 8.1 %conditional.11 = ((f32[8,3,256]{2,1,0:T(4,128)S(1)}, f32[8,3,256]{2,1,0:T(4,128)S(1)}, f32[8,3,256,128]{3,2,1,0:T(8,128)S(1)})) conditional(s32[]{:T(128)} %convert_element_type.119, (f32[8,3,256]{2,1,0:T(4,128)S(1)}, f32[8,3,256]{2,1,0:T(4,128)S(1)}, f32[8,3,256,128]{3,2,1,0:T(8,128)S(1)}) %tuple.281, (s32[]{:T(128)}, s32[256]{0:T(256)S(1)}, ...), branch_computations={%region_9.9_spmd, %region_10.12_spmd} | conditional | flops 824390144 | bytes 30548058 | solution.py:61
  202.4 8.1 %conditional.11 = ((f32[8,3,256]{2,1,0:T(4,128)S(1)}, f32[8,3,256]{2,1,0:T(4,128)S(1)}, f32[8,3,256,128]{3,2,1,0:T(8,128)S(1)})) conditional(s32[]{:T(128)} %convert_element_type.119, (f32[8,3,256]{2,1,0:T(4,128)S(1)}, f32[8,3,256]{2,1,0:T(4,128)S(1)}, f32[8,3,256,128]{3,2,1,0:T(8,128)S(1)}) %tuple.281, (s32[]{:T(128)}, s32[256]{0:T(256)S(1)}, ...), branch_computations={%region_9.9_spmd, %region_10.12_spmd} | conditional | flops 824390144 | bytes 30548058 | solution.py:61
  210.5 22.6 %while.97 = (s32[]{:T(128)}, f32[8,3,256]{2,1,0:T(4,128)S(1)}, f32[8,3,256]{2,1,0:T(4,128)S(1)}, f32[8,3,256,128]{3,2,1,0:T(8,128)S(1)}, s32[]{:T(128)}, /*index...) while((s32[]{:T(128)}, f32[8,3,256]{2,1,0:T(4,128)S(1)}, ...), condition=%wide.region_19.20_spmd, body=%wide.region_14.19_spmd.sunk | while | flops 824390144 | bytes 30551492 | solution.py:73
  213.8 8.1 %conditional.12 = ((f32[8,3,256]{2,1,0:T(4,128)S(1)}, f32[8,3,256]{2,1,0:T(4,128)S(1)}, f32[8,3,256,128]{3,2,1,0:T(8,128)S(1)})) conditional(s32[]{:T(128)} %convert_element_type.120, (f32[8,3,256]{2,1,0:T(4,128)S(1)}, f32[8,3,256]{2,1,0:T(4,128)S(1)}, f32[8,3,256,128]{3,2,1,0:T(8,128)S(1)}) %tuple.284, (s32[]{:T(128)}, s32[256]{0:T(256)S(1)}, ...), branch_computations={%region_15.15_spmd, %region_16.18_spmd} | conditional | flops 824390144 | bytes 30548058 | solution.py:61
  225.0 8.1 %conditional.12 = ((f32[8,3,256]{2,1,0:T(4,128)S(1)}, f32[8,3,256]{2,1,0:T(4,128)S(1)}, f32[8,3,256,128]{3,2,1,0:T(8,128)S(1)})) conditional(s32[]{:T(128)} %convert_element_type.120, (f32[8,3,256]{2,1,0:T(4,128)S(1)}, f32[8,3,256]{2,1,0:T(4,128)S(1)}, f32[8,3,256,128]{3,2,1,0:T(8,128)S(1)}) %tuple.284, (s32[]{:T(128)}, s32[256]{0:T(256)S(1)}, ...), branch_computations={%region_15.15_spmd, %region_16.18_spmd} | conditional | flops 824390144 | bytes 30548058 | solution.py:61
  233.1 22.6 %while.98 = (s32[]{:T(128)}, f32[8,3,256]{2,1,0:T(4,128)S(1)}, f32[8,3,256]{2,1,0:T(4,128)S(1)}, f32[8,3,256,128]{3,2,1,0:T(8,128)S(1)}, s32[]{:T(128)}, /*index...) while((s32[]{:T(128)}, f32[8,3,256]{2,1,0:T(4,128)S(1)}, ...), condition=%wide.region_25.26_spmd, body=%wide.region_20.25_spmd.sunk | while | flops 824390144 | bytes 30551492 | solution.py:73
  236.3 8.1 %conditional.13 = ((f32[8,3,256]{2,1,0:T(4,128)S(1)}, f32[8,3,256]{2,1,0:T(4,128)S(1)}, f32[8,3,256,128]{3,2,1,0:T(8,128)S(1)})) conditional(s32[]{:T(128)} %convert_element_type.121, (f32[8,3,256]{2,1,0:T(4,128)S(1)}, f32[8,3,256]{2,1,0:T(4,128)S(1)}, f32[8,3,256,128]{3,2,1,0:T(8,128)S(1)}) %tuple.287, (s32[]{:T(128)}, s32[256]{0:T(256)S(1)}, ...), branch_computations={%region_21.21_spmd, %region_22.24_spmd} | conditional | flops 824390144 | bytes 30548058 | solution.py:61
  247.7 8.1 %conditional.13 = ((f32[8,3,256]{2,1,0:T(4,128)S(1)}, f32[8,3,256]{2,1,0:T(4,128)S(1)}, f32[8,3,256,128]{3,2,1,0:T(8,128)S(1)})) conditional(s32[]{:T(128)} %convert_element_type.121, (f32[8,3,256]{2,1,0:T(4,128)S(1)}, f32[8,3,256]{2,1,0:T(4,128)S(1)}, f32[8,3,256,128]{3,2,1,0:T(8,128)S(1)}) %tuple.287, (s32[]{:T(128)}, s32[256]{0:T(256)S(1)}, ...), branch_computations={%region_21.21_spmd, %region_22.24_spmd} | conditional | flops 824390144 | bytes 30548058 | solution.py:61
  255.8 14.8 %while.99 = (s32[]{:T(128)}, f32[8,3,256]{2,1,0:T(4,128)S(1)}, f32[8,3,256]{2,1,0:T(4,128)S(1)}, f32[8,3,256,128]{3,2,1,0:T(8,128)S(1)}, s32[]{:T(128)}, /*index...) while((s32[]{:T(128)}, f32[8,3,256]{2,1,0:T(4,128)S(1)}, ...), condition=%wide.region_31.32_spmd, body=%wide.region_26.31_spmd.sunk | while | flops 824390144 | bytes 30551492 | solution.py:73
  262.5 8.1 %conditional.14 = ((f32[8,3,256]{2,1,0:T(4,128)S(1)}, f32[8,3,256]{2,1,0:T(4,128)S(1)}, f32[8,3,256,128]{3,2,1,0:T(8,128)S(1)})) conditional(s32[]{:T(128)} %convert_element_type.122, (f32[8,3,256]{2,1,0:T(4,128)S(1)}, f32[8,3,256]{2,1,0:T(4,128)S(1)}, f32[8,3,256,128]{3,2,1,0:T(8,128)S(1)}) %tuple.290, (s32[]{:T(128)}, s32[256]{0:T(256)S(1)}, ...), branch_computations={%region_27.27_spmd, %region_28.30_spmd} | conditional | flops 824390144 | bytes 30548058 | solution.py:61
  (143 shorter events, 117.7 us)
Async XLA Ops:
  6.5 19.2 %all-gather.3.cloned.1.call-start = ((), (), s32[]{:S(2)}) async-start(), calls=%async_computation | async-start | bytes 1572864 | tf_op jit(solution)/shard_map/all_gather | solution.py:93
  8.6 34.4 %all-gather.5.cloned.1.call-start = ((), (), s32[]{:S(2)}) async-start(), calls=%async_computation.1 | async-start | bytes 1572864 | tf_op jit(solution)/shard_map/all_gather | solution.py:94
  25.8 28.1 %collective-permute-start = (bf16[512,1024]{0,1:T(8,128)(2,1)}, bf16[512,1024]{0,1:T(8,128)(2,1)S(1)}, u32[]{:S(2)}, u32[]{:S(2)}) collective-permute-start(bf16[512,1024]{0,1:T(8,128)(2,1)} %all-gather.3.cloned.1.call-done), channel_id=1, source_target_pairs={{0,2},{2,4},{4,6},{6,8},{8,10},{10,12},{12,14},{14,16},{16,18},{18... | collective-permute-start | bytes 3145736 | tf_op jit(solution)/shard_map/ppermute | solution.py:15
  43.0 33.3 %collective-permute-start.1 = (bf16[512,1024]{0,1:T(8,128)(2,1)}, bf16[512,1024]{0,1:T(8,128)(2,1)S(1)}, u32[]{:S(2)}, u32[]{:S(2)}) collective-permute-start(bf16[512,1024]{0,1:T(8,128)(2,1)} %all-gather.5.cloned.1.call-done), channel_id=1, source_target_pairs={{0,2},{2,4},{4,6},{6,8},{8,10},{10,12},{12,14},{14,16},{16,18},{18... | collective-permute-start | bytes 3145736 | tf_op jit(solution)/shard_map/ppermute | solution.py:15
  53.9 73.0 %copy-start.2 = (bf16[512,1024]{0,1:T(8,128)(2,1)}, bf16[512,1024]{0,1:T(8,128)(2,1)S(1)}, u32[]{:S(2)}) copy-start(bf16[512,1024]{0,1:T(8,128)(2,1)S(1)} %collective-permute-done) | copy-start | bytes 3145732
  53.9 44.9 %collective-permute-start.2 = (bf16[512,1024]{0,1:T(8,128)(2,1)S(1)}, bf16[512,1024]{0,1:T(8,128)(2,1)S(1)}, u32[]{:S(2)}, u32[]{:S(2)}) collective-permute-start(bf16[512,1024]{0,1:T(8,128)(2,1)S(1)} %collective-permute-done), channel_id=1, source_target_pairs={{0,2},{2,4},{4,6},{6,8},{8,10},{10,12},{12,14},{14,16},{16,18},{18... | collective-permute-start | bytes 3145736 | tf_op jit(solution)/shard_map/ppermute | solution.py:15
  76.3 22.5 %copy-start.3 = (bf16[512,1024]{0,1:T(8,128)(2,1)}, bf16[512,1024]{0,1:T(8,128)(2,1)S(1)}, u32[]{:S(2)}) copy-start(bf16[512,1024]{0,1:T(8,128)(2,1)S(1)} %collective-permute-done.1) | copy-start | bytes 3145732
  76.3 45.0 %collective-permute-start.3 = (bf16[512,1024]{0,1:T(8,128)(2,1)S(1)}, bf16[512,1024]{0,1:T(8,128)(2,1)}, u32[]{:S(2)}, u32[]{:S(2)}) collective-permute-start(bf16[512,1024]{0,1:T(8,128)(2,1)S(1)} %collective-permute-done.1), channel_id=1, source_target_pairs={{0,2},{2,4},{4,6},{6,8},{8,10},{10,12},{12,14},{14,16},{16,18},{18... | collective-permute-start | bytes 3145736 | tf_op jit(solution)/shard_map/ppermute | solution.py:15
  98.8 33.0 %copy-start.1 = (bf16[512,1024]{0,1:T(8,128)(2,1)}, bf16[512,1024]{0,1:T(8,128)(2,1)S(1)}, u32[]{:S(2)}) copy-start(bf16[512,1024]{0,1:T(8,128)(2,1)S(1)} %collective-permute-done.2) | copy-start | bytes 3145732
  98.8 45.0 %collective-permute-start.4 = (bf16[512,1024]{0,1:T(8,128)(2,1)S(1)}, bf16[512,1024]{0,1:T(8,128)(2,1)}, u32[]{:S(2)}, u32[]{:S(2)}) collective-permute-start(bf16[512,1024]{0,1:T(8,128)(2,1)S(1)} %collective-permute-done.2), channel_id=1, source_target_pairs={{0,2},{2,4},{4,6},{6,8},{8,10},{10,12},{12,14},{14,16},{16,18},{18... | collective-permute-start | bytes 3145736 | tf_op jit(solution)/shard_map/ppermute | solution.py:15
  121.4 44.9 %collective-permute-start.5 = (bf16[512,1024]{0,1:T(8,128)(2,1)}, bf16[512,1024]{0,1:T(8,128)(2,1)}, u32[]{:S(2)}, u32[]{:S(2)}) collective-permute-start(bf16[512,1024]{0,1:T(8,128)(2,1)} %collective-permute-done.3), channel_id=1, source_target_pairs={{0,2},{2,4},{4,6},{6,8},{8,10},{10,12},{12,14},{14,16},{16,18},{18... | collective-permute-start | bytes 3145736 | tf_op jit(solution)/shard_map/ppermute | solution.py:15
  131.9 40.1 %copy-start = (f32[8,256,256,3]{2,1,3,0:T(8,128)}, f32[8,256,256,3]{2,1,3,0:T(8,128)S(1)}, u32[]{:S(2)}) copy-start(f32[8,256,256,3]{2,1,3,0:T(8,128)S(1)} %get-tuple-element.2461) | copy-start | bytes 18874372
  131.9 43.1 %copy-start.4 = (bf16[256,1024]{1,0:T(8,128)(2,1)S(1)}, bf16[256,1024]{1,0:T(8,128)(2,1)}, u32[]{:S(2)}) copy-start(bf16[256,1024]{1,0:T(8,128)(2,1)} %param.26) | copy-start | bytes 1572868
  143.9 111.9 %collective-permute-start.6 = (bf16[512,1024]{0,1:T(8,128)(2,1)}, bf16[512,1024]{0,1:T(8,128)(2,1)}, u32[]{:S(2)}, u32[]{:S(2)}) collective-permute-start(bf16[512,1024]{0,1:T(8,128)(2,1)} %collective-permute-done.4), channel_id=1, source_target_pairs={{0,2},{2,4},{4,6},{6,8},{8,10},{10,12},{12,14},{14,16},{16,18},{18... | collective-permute-start | bytes 3145736 | tf_op jit(solution)/shard_map/ppermute | solution.py:15
  166.3 89.4 %collective-permute-start.7 = (bf16[512,1024]{0,1:T(8,128)(2,1)}, bf16[512,1024]{0,1:T(8,128)(2,1)}, u32[]{:S(2)}, u32[]{:S(2)}) collective-permute-start(bf16[512,1024]{0,1:T(8,128)(2,1)} %collective-permute-done.5), channel_id=1, source_target_pairs={{0,2},{2,4},{4,6},{6,8},{8,10},{10,12},{12,14},{14,16},{16,18},{18... | collective-permute-start | bytes 3145736 | tf_op jit(solution)/shard_map/ppermute | solution.py:15
Sparse Core Ops, SparseCore 0:
  9.1 16.5 all-gather.2
  27.5 15.4 all-gather.4
where the time goes:
time: 285 us; the launch traced here: 284 us
  waiting for transfers between devices  116 us (41%)
  matrix products  42.7 us (15%)
  local copies, waits for them, and re-layouts  42.6 us (15%)
  starting transfers between devices  39.8 us (14%)
  other arithmetic  14.6 us (5%)
  loops' own time  14 us (5%)
  between operations  13.6 us (5%)
    ppermute x8, waiting for transfers between devices, passed_along(): return lax.ppermute(block, axis, route)  87.5 us
    ppermute x8, starting transfers between devices, passed_along(): return lax.ppermute(block, axis, route)  39.8 us
    dot_general x8, matrix products, fold_piece(): jnp.einsum('grqk,kgd->grqd', weights.astype(jnp.bfloat16), value_heads, p...  23 us
    dot_general x8, matrix products, fold_piece(): jnp.einsum('qgrd,kgd->grqk', query_rows, key_heads, preferred_element_typ...  19.7 us
    all_gather x1, waiting for transfers between devices, shards(): lax.all_gather(keys, 'attn', axis=0, tiled=True)  15 us
    all_gather x1, waiting for transfers between devices, shards(): lax.all_gather(values, 'attn', axis=0, tiled=True)  13.9 us
    another operation x5, loops' own time, fold_window(): return lax.fori_loop(0, pieces, one_piece, carry)  13.5 us
    reduce_sum x8, other arithmetic, fold_piece(): total = total * rescale + jnp.sum(weights, axis=-1)  10.9 us
  transfers between devices with their start and end apart: 10, of which 8 were waited for; matrix products, arithmetic and copies ran while one was open for 28% of the time, Pallas kernels for 0%

commit v1 on v0

--- a/solution.py
+++ b/solution.py
@@ -90,7 +90,9 @@
     )
     carry = fold_piece(carry, query_rows, keys, values, query_pos, query_doc, query_pos, query_doc)
     window = (
-        lax.all_gather(keys, "attn", axis=0, tiled=True),
+        jnp.concatenate(
+            lax.all_to_all(jnp.stack([keys] * lax.axis_size("attn")), "attn", 0, 0), axis=0
+        ),
         lax.all_gather(values, "attn", axis=0, tiled=True),
     )
     carry = fold_window(carry, context, window[0], window[1], chip * cores)

time: 285 us -> 274 us (0.961)
  waiting for transfers between devices: 116 us -> 100 us
  blocking collectives: 0 us -> 4.58 us
    all_gather x1 -> x0, waiting for transfers between devices: 15 us -> none  [shards(): lax.all_gather(keys, 'attn', axis=0, tiled=True)]
    all_gather x1, waiting for transfers between devices: 13.9 us -> 7.25 us  [shards(): lax.all_gather(values, 'attn', axis=0, tiled=True)]
    ppermute x8, waiting for transfers between devices: 87.5 us -> 93 us  [passed_along(): return lax.ppermute(block, axis, route)]
    all_to_all x0 -> x1, blocking collectives: none -> 4.58 us  [shards(): lax.all_to_all(jnp.stack([keys] * lax.axis_size('attn')), 'attn', 0, 0)]
    unnamed x15 -> x16, local copies, waits for them, and re-layouts: 7.86 us -> 5.63 us
  transfers between devices with their start and end apart: 10 -> 9, of which waited for: 8 -> 7; matrix products, arithmetic and copies ran while one was open for 28% -> 29% of each run, Pallas kernels for 0% -> 0%
where the time goes in v1:
time: 274 us; the launch traced here: 273 us
  waiting for transfers between devices  100 us (36%)
  matrix products  43.7 us (16%)
  local copies, waits for them, and re-layouts  40.9 us (15%)
  starting transfers between devices  39.9 us (15%)
  other arithmetic  15.9 us (6%)
  loops' own time  14 us (5%)
  between operations  13.6 us (5%)
  blocking collectives  4.58 us (2%)
    ppermute x8, waiting for transfers between devices, passed_along(): return lax.ppermute(block, axis, route)  93 us
    ppermute x8, starting transfers between devices, passed_along(): return lax.ppermute(block, axis, route)  39.9 us
    dot_general x8, matrix products, fold_piece(): jnp.einsum('grqk,kgd->grqd', weights.astype(jnp.bfloat16), value_heads, p...  23 us
    dot_general x8, matrix products, fold_piece(): jnp.einsum('qgrd,kgd->grqk', query_rows, key_heads, preferred_element_typ...  20.7 us
    another operation x5, loops' own time, fold_window(): return lax.fori_loop(0, pieces, one_piece, carry)  13.4 us
    reduce_sum x8, other arithmetic, fold_piece(): total = total * rescale + jnp.sum(weights, axis=-1)  10.9 us
    dynamic_slice x7, local copies, waits for them, and re-layouts, one_piece(): lax.dynamic_slice_in_dim(window_values, piece_num * rows, rows, 0)  8.92 us
    dynamic_slice x10, local copies, waits for them, and re-layouts, fold_remote(): key_doc = lax.dynamic_slice_in_dim(doc_ids, jnp.maximum(first, 0), rows)  7.78 us
  transfers between devices with their start and end apart: 9, of which 7 were waited for; matrix products, arithmetic and copies ran while one was open for 29% of the time, Pallas kernels for 0%

profile of v1, /device:TPU:46, one launch (start us, length us, event | category | flops | bytes accessed | tf_op | source)
XLA Modules:
  0.0 272.9 jit_solution(16235063923042756431)
XLA Ops:
  18.5 7.3 %all-gather.2.cloned.1.call-done = bf16[512,1024]{0,1:T(8,128)(2,1)} async-done(((bf16[256,1024]{0,1:T(8,128)(2,1)}), bf16[512,1024]{0,1:T(8,128)(2,1)}) %all-gather.2.cloned.1.call-update) | async-done | bytes 1048592 | tf_op jit(solution)/shard_map/all_gather | solution.py:96
  29.1 14.0 %collective-permute-done = bf16[512,1024]{0,1:T(8,128)(2,1)} collective-permute-done((bf16[512,1024]{0,1:T(8,128)(2,1)S(1)}, bf16[512,1024]{0,1:T(8,128)(2,1)}, u32[]{:S(2)}, u32[]{:S(2)}) %collective-permute-start) | collective-permute-done | bytes 1048608 | tf_op jit(solution)/shard_map/ppermute | solution.py:15
  48.6 16.9 %collective-permute-done.1 = bf16[512,1024]{0,1:T(8,128)(2,1)S(1)} collective-permute-done((bf16[512,1024]{0,1:T(8,128)(2,1)}, bf16[512,1024]{0,1:T(8,128)(2,1)S(1)}, u32[]{:S(2)}, u32[]{:S(2)}) %collective-permute-start.1) | collective-permute-done | bytes 1048608 | tf_op jit(solution)/shard_map/ppermute | solution.py:15
  65.5 5.5 %collective-permute-start.3 = (bf16[512,1024]{0,1:T(8,128)(2,1)S(1)}, bf16[512,1024]{0,1:T(8,128)(2,1)}, u32[]{:S(2)}, u32[]{:S(2)}) collective-permute-start(bf16[512,1024]{0,1:T(8,128)(2,1)S(1)} %collective-permute-done.1), channel_id=1, source_target_pairs={{0,2},{2,4},{4,6},{6,8},{8,10},{10,12},{12,14},{14,16},{16,18},{18... | collective-permute-start | bytes 3145736 | tf_op jit(solution)/shard_map/ppermute | solution.py:15
  71.0 17.0 %collective-permute-done.2 = bf16[512,1024]{0,1:T(8,128)(2,1)S(1)} collective-permute-done((bf16[512,1024]{0,1:T(8,128)(2,1)}, bf16[512,1024]{0,1:T(8,128)(2,1)S(1)}, u32[]{:S(2)}, u32[]{:S(2)}) %collective-permute-start.2) | collective-permute-done | bytes 1048608 | tf_op jit(solution)/shard_map/ppermute | solution.py:15
  88.0 5.5 %collective-permute-start.4 = (bf16[512,1024]{0,1:T(8,128)(2,1)S(1)}, bf16[512,1024]{0,1:T(8,128)(2,1)}, u32[]{:S(2)}, u32[]{:S(2)}) collective-permute-start(bf16[512,1024]{0,1:T(8,128)(2,1)S(1)} %collective-permute-done.2), channel_id=1, source_target_pairs={{0,2},{2,4},{4,6},{6,8},{8,10},{10,12},{12,14},{14,16},{16,18},{18... | collective-permute-start | bytes 3145736 | tf_op jit(solution)/shard_map/ppermute | solution.py:15
  93.5 17.1 %collective-permute-done.3 = bf16[512,1024]{0,1:T(8,128)(2,1)} collective-permute-done((bf16[512,1024]{0,1:T(8,128)(2,1)S(1)}, bf16[512,1024]{0,1:T(8,128)(2,1)}, u32[]{:S(2)}, u32[]{:S(2)}) %collective-permute-start.3) | collective-permute-done | bytes 1048608 | tf_op jit(solution)/shard_map/ppermute | solution.py:15
  110.5 5.5 %collective-permute-start.5 = (bf16[512,1024]{0,1:T(8,128)(2,1)}, bf16[512,1024]{0,1:T(8,128)(2,1)}, u32[]{:S(2)}, u32[]{:S(2)}) collective-permute-start(bf16[512,1024]{0,1:T(8,128)(2,1)} %collective-permute-done.3), channel_id=1, source_target_pairs={{0,2},{2,4},{4,6},{6,8},{8,10},{10,12},{12,14},{14,16},{16,18},{18... | collective-permute-start | bytes 3145736 | tf_op jit(solution)/shard_map/ppermute | solution.py:15
  121.8 11.2 %collective-permute-done.4 = bf16[512,1024]{0,1:T(8,128)(2,1)} collective-permute-done((bf16[512,1024]{0,1:T(8,128)(2,1)S(1)}, bf16[512,1024]{0,1:T(8,128)(2,1)}, u32[]{:S(2)}, u32[]{:S(2)}) %collective-permute-start.4) | collective-permute-done | bytes 1048608 | tf_op jit(solution)/shard_map/ppermute | solution.py:15
  133.0 5.5 %collective-permute-start.6 = (bf16[512,1024]{0,1:T(8,128)(2,1)}, bf16[512,1024]{0,1:T(8,128)(2,1)}, u32[]{:S(2)}, u32[]{:S(2)}) collective-permute-start(bf16[512,1024]{0,1:T(8,128)(2,1)} %collective-permute-done.4), channel_id=1, source_target_pairs={{0,2},{2,4},{4,6},{6,8},{8,10},{10,12},{12,14},{14,16},{16,18},{18... | collective-permute-start | bytes 3145736 | tf_op jit(solution)/shard_map/ppermute | solution.py:15
  138.5 17.0 %collective-permute-done.5 = bf16[512,1024]{0,1:T(8,128)(2,1)} collective-permute-done((bf16[512,1024]{0,1:T(8,128)(2,1)}, bf16[512,1024]{0,1:T(8,128)(2,1)}, u32[]{:S(2)}, u32[]{:S(2)}) %collective-permute-start.5) | collective-permute-done | bytes 1048608 | tf_op jit(solution)/shard_map/ppermute | solution.py:15
  155.5 5.7 %collective-permute-start.7 = (bf16[512,1024]{0,1:T(8,128)(2,1)}, bf16[512,1024]{0,1:T(8,128)(2,1)}, u32[]{:S(2)}, u32[]{:S(2)}) collective-permute-start(bf16[512,1024]{0,1:T(8,128)(2,1)} %collective-permute-done.5), channel_id=1, source_target_pairs={{0,2},{2,4},{4,6},{6,8},{8,10},{10,12},{12,14},{14,16},{16,18},{18... | collective-permute-start | bytes 3145736 | tf_op jit(solution)/shard_map/ppermute | solution.py:15
  170.2 6.4 %while.95 = (s32[]{:T(128)}, f32[8,3,256]{2,1,0:T(4,128)S(1)}, f32[8,3,256]{2,1,0:T(4,128)S(1)}, f32[8,3,256,128]{3,2,1,0:T(8,128)S(1)}, s32[]{:T(128)}, /*index...) while((s32[]{:T(128)}, f32[8,3,256]{2,1,0:T(4,128)S(1)}, ...), condition=%wide.region_7.8_spmd, body=%wide.region_2.7_spmd.sunk | while | flops 824390144 | bytes 30551492 | solution.py:73
  176.6 22.6 %while.96 = (s32[]{:T(128)}, f32[8,3,256]{2,1,0:T(4,128)S(1)}, f32[8,3,256]{2,1,0:T(4,128)S(1)}, f32[8,3,256,128]{3,2,1,0:T(8,128)S(1)}, s32[]{:T(128)}, /*index...) while((s32[]{:T(128)}, f32[8,3,256]{2,1,0:T(4,128)S(1)}, ...), condition=%wide.region_13.14_spmd, body=%wide.region_8.13_spmd.sunk | while | flops 824390144 | bytes 30551492 | solution.py:73
  179.8 8.1 %conditional.11 = ((f32[8,3,256]{2,1,0:T(4,128)S(1)}, f32[8,3,256]{2,1,0:T(4,128)S(1)}, f32[8,3,256,128]{3,2,1,0:T(8,128)S(1)})) conditional(s32[]{:T(128)} %convert_element_type.119, (f32[8,3,256]{2,1,0:T(4,128)S(1)}, f32[8,3,256]{2,1,0:T(4,128)S(1)}, f32[8,3,256,128]{3,2,1,0:T(8,128)S(1)}) %tuple.281, (s32[]{:T(128)}, s32[256]{0:T(256)S(1)}, ...), branch_computations={%region_9.9_spmd, %region_10.12_spmd} | conditional | flops 824390144 | bytes 30548058 | solution.py:61
  191.1 8.1 %conditional.11 = ((f32[8,3,256]{2,1,0:T(4,128)S(1)}, f32[8,3,256]{2,1,0:T(4,128)S(1)}, f32[8,3,256,128]{3,2,1,0:T(8,128)S(1)})) conditional(s32[]{:T(128)} %convert_element_type.119, (f32[8,3,256]{2,1,0:T(4,128)S(1)}, f32[8,3,256]{2,1,0:T(4,128)S(1)}, f32[8,3,256,128]{3,2,1,0:T(8,128)S(1)}) %tuple.281, (s32[]{:T(128)}, s32[256]{0:T(256)S(1)}, ...), branch_computations={%region_9.9_spmd, %region_10.12_spmd} | conditional | flops 824390144 | bytes 30548058 | solution.py:61
  199.2 22.6 %while.97 = (s32[]{:T(128)}, f32[8,3,256]{2,1,0:T(4,128)S(1)}, f32[8,3,256]{2,1,0:T(4,128)S(1)}, f32[8,3,256,128]{3,2,1,0:T(8,128)S(1)}, s32[]{:T(128)}, /*index...) while((s32[]{:T(128)}, f32[8,3,256]{2,1,0:T(4,128)S(1)}, ...), condition=%wide.region_19.20_spmd, body=%wide.region_14.19_spmd.sunk | while | flops 824390144 | bytes 30551492 | solution.py:73
  202.5 8.1 %conditional.12 = ((f32[8,3,256]{2,1,0:T(4,128)S(1)}, f32[8,3,256]{2,1,0:T(4,128)S(1)}, f32[8,3,256,128]{3,2,1,0:T(8,128)S(1)})) conditional(s32[]{:T(128)} %convert_element_type.120, (f32[8,3,256]{2,1,0:T(4,128)S(1)}, f32[8,3,256]{2,1,0:T(4,128)S(1)}, f32[8,3,256,128]{3,2,1,0:T(8,128)S(1)}) %tuple.284, (s32[]{:T(128)}, s32[256]{0:T(256)S(1)}, ...), branch_computations={%region_15.15_spmd, %region_16.18_spmd} | conditional | flops 824390144 | bytes 30548058 | solution.py:61
  213.7 8.1 %conditional.12 = ((f32[8,3,256]{2,1,0:T(4,128)S(1)}, f32[8,3,256]{2,1,0:T(4,128)S(1)}, f32[8,3,256,128]{3,2,1,0:T(8,128)S(1)})) conditional(s32[]{:T(128)} %convert_element_type.120, (f32[8,3,256]{2,1,0:T(4,128)S(1)}, f32[8,3,256]{2,1,0:T(4,128)S(1)}, f32[8,3,256,128]{3,2,1,0:T(8,128)S(1)}) %tuple.284, (s32[]{:T(128)}, s32[256]{0:T(256)S(1)}, ...), branch_computations={%region_15.15_spmd, %region_16.18_spmd} | conditional | flops 824390144 | bytes 30548058 | solution.py:61
  221.8 22.8 %while.98 = (s32[]{:T(128)}, f32[8,3,256]{2,1,0:T(4,128)S(1)}, f32[8,3,256]{2,1,0:T(4,128)S(1)}, f32[8,3,256,128]{3,2,1,0:T(8,128)S(1)}, s32[]{:T(128)}, /*index...) while((s32[]{:T(128)}, f32[8,3,256]{2,1,0:T(4,128)S(1)}, ...), condition=%wide.region_25.26_spmd, body=%wide.region_20.25_spmd.sunk | while | flops 824390144 | bytes 30551492 | solution.py:73
  225.2 8.1 %conditional.13 = ((f32[8,3,256]{2,1,0:T(4,128)S(1)}, f32[8,3,256]{2,1,0:T(4,128)S(1)}, f32[8,3,256,128]{3,2,1,0:T(8,128)S(1)})) conditional(s32[]{:T(128)} %convert_element_type.121, (f32[8,3,256]{2,1,0:T(4,128)S(1)}, f32[8,3,256]{2,1,0:T(4,128)S(1)}, f32[8,3,256,128]{3,2,1,0:T(8,128)S(1)}) %tuple.287, (s32[]{:T(128)}, s32[256]{0:T(256)S(1)}, ...), branch_computations={%region_21.21_spmd, %region_22.24_spmd} | conditional | flops 824390144 | bytes 30548058 | solution.py:61
  236.6 8.1 %conditional.13 = ((f32[8,3,256]{2,1,0:T(4,128)S(1)}, f32[8,3,256]{2,1,0:T(4,128)S(1)}, f32[8,3,256,128]{3,2,1,0:T(8,128)S(1)})) conditional(s32[]{:T(128)} %convert_element_type.121, (f32[8,3,256]{2,1,0:T(4,128)S(1)}, f32[8,3,256]{2,1,0:T(4,128)S(1)}, f32[8,3,256,128]{3,2,1,0:T(8,128)S(1)}) %tuple.287, (s32[]{:T(128)}, s32[256]{0:T(256)S(1)}, ...), branch_computations={%region_21.21_spmd, %region_22.24_spmd} | conditional | flops 824390144 | bytes 30548058 | solution.py:61
  244.7 15.0 %while.99 = (s32[]{:T(128)}, f32[8,3,256]{2,1,0:T(4,128)S(1)}, f32[8,3,256]{2,1,0:T(4,128)S(1)}, f32[8,3,256,128]{3,2,1,0:T(8,128)S(1)}, s32[]{:T(128)}, /*index...) while((s32[]{:T(128)}, f32[8,3,256]{2,1,0:T(4,128)S(1)}, ...), condition=%wide.region_31.32_spmd, body=%wide.region_26.31_spmd.sunk | while | flops 824390144 | bytes 30551492 | solution.py:73
  251.6 8.1 %conditional.14 = ((f32[8,3,256]{2,1,0:T(4,128)S(1)}, f32[8,3,256]{2,1,0:T(4,128)S(1)}, f32[8,3,256,128]{3,2,1,0:T(8,128)S(1)})) conditional(s32[]{:T(128)} %convert_element_type.122, (f32[8,3,256]{2,1,0:T(4,128)S(1)}, f32[8,3,256]{2,1,0:T(4,128)S(1)}, f32[8,3,256,128]{3,2,1,0:T(8,128)S(1)}) %tuple.290, (s32[]{:T(128)}, s32[256]{0:T(256)S(1)}, ...), branch_computations={%region_27.27_spmd, %region_28.30_spmd} | conditional | flops 824390144 | bytes 30548058 | solution.py:61
  (144 shorter events, 117.4 us)
Async XLA Ops:
  6.5 111.2 %copy-start.4 = (bf16[256,1024]{1,0:T(8,128)(2,1)S(1)}, bf16[256,1024]{1,0:T(8,128)(2,1)}, u32[]{:S(2)}) copy-start(bf16[256,1024]{1,0:T(8,128)(2,1)} %param.25) | copy-start | bytes 1572868
  6.5 19.2 %all-gather.2.cloned.1.call-start = ((), (), s32[]{:S(2)}) async-start(), calls=%async_computation.1 | async-start | bytes 1572864 | tf_op jit(solution)/shard_map/all_gather | solution.py:96
  15.1 101.0 %copy-start.1 = (bf16[512,1024]{0,1:T(8,128)(2,1)}, bf16[512,1024]{0,1:T(8,128)(2,1)S(1)}, u32[]{:S(2)}) copy-start(bf16[512,1024]{0,1:T(8,128)(2,1)S(1)} %copy.86) | copy-start | bytes 3145732
  15.1 28.0 %collective-permute-start = (bf16[512,1024]{0,1:T(8,128)(2,1)S(1)}, bf16[512,1024]{0,1:T(8,128)(2,1)}, u32[]{:S(2)}, u32[]{:S(2)}) collective-permute-start(bf16[512,1024]{0,1:T(8,128)(2,1)S(1)} %copy.86), channel_id=1, source_target_pairs={{0,2},{2,4},{4,6},{6,8},{8,10},{10,12},{12,14},{14,16},{16,18},{18... | collective-permute-start | bytes 3145736 | tf_op jit(solution)/shard_map/ppermute | solution.py:15
  25.8 39.7 %collective-permute-start.1 = (bf16[512,1024]{0,1:T(8,128)(2,1)}, bf16[512,1024]{0,1:T(8,128)(2,1)S(1)}, u32[]{:S(2)}, u32[]{:S(2)}) collective-permute-start(bf16[512,1024]{0,1:T(8,128)(2,1)} %all-gather.2.cloned.1.call-done), channel_id=1, source_target_pairs={{0,2},{2,4},{4,6},{6,8},{8,10},{10,12},{12,14},{14,16},{16,18},{18... | collective-permute-start | bytes 3145736 | tf_op jit(solution)/shard_map/ppermute | solution.py:15
  43.1 44.8 %collective-permute-start.2 = (bf16[512,1024]{0,1:T(8,128)(2,1)}, bf16[512,1024]{0,1:T(8,128)(2,1)S(1)}, u32[]{:S(2)}, u32[]{:S(2)}) collective-permute-start(bf16[512,1024]{0,1:T(8,128)(2,1)} %collective-permute-done), channel_id=1, source_target_pairs={{0,2},{2,4},{4,6},{6,8},{8,10},{10,12},{12,14},{14,16},{16,18},{18... | collective-permute-start | bytes 3145736 | tf_op jit(solution)/shard_map/ppermute | solution.py:15
  65.5 22.5 %copy-start.3 = (bf16[512,1024]{0,1:T(8,128)(2,1)}, bf16[512,1024]{0,1:T(8,128)(2,1)S(1)}, u32[]{:S(2)}) copy-start(bf16[512,1024]{0,1:T(8,128)(2,1)S(1)} %collective-permute-done.1) | copy-start | bytes 3145732
  65.5 45.0 %collective-permute-start.3 = (bf16[512,1024]{0,1:T(8,128)(2,1)S(1)}, bf16[512,1024]{0,1:T(8,128)(2,1)}, u32[]{:S(2)}, u32[]{:S(2)}) collective-permute-start(bf16[512,1024]{0,1:T(8,128)(2,1)S(1)} %collective-permute-done.1), channel_id=1, source_target_pairs={{0,2},{2,4},{4,6},{6,8},{8,10},{10,12},{12,14},{14,16},{16,18},{18... | collective-permute-start | bytes 3145736 | tf_op jit(solution)/shard_map/ppermute | solution.py:15
  88.0 33.8 %copy-start.2 = (bf16[512,1024]{0,1:T(8,128)(2,1)}, bf16[512,1024]{0,1:T(8,128)(2,1)S(1)}, u32[]{:S(2)}) copy-start(bf16[512,1024]{0,1:T(8,128)(2,1)S(1)} %collective-permute-done.2) | copy-start | bytes 3145732
  88.0 45.0 %collective-permute-start.4 = (bf16[512,1024]{0,1:T(8,128)(2,1)S(1)}, bf16[512,1024]{0,1:T(8,128)(2,1)}, u32[]{:S(2)}, u32[]{:S(2)}) collective-permute-start(bf16[512,1024]{0,1:T(8,128)(2,1)S(1)} %collective-permute-done.2), channel_id=1, source_target_pairs={{0,2},{2,4},{4,6},{6,8},{8,10},{10,12},{12,14},{14,16},{16,18},{18... | collective-permute-start | bytes 3145736 | tf_op jit(solution)/shard_map/ppermute | solution.py:15
  110.5 44.9 %collective-permute-start.5 = (bf16[512,1024]{0,1:T(8,128)(2,1)}, bf16[512,1024]{0,1:T(8,128)(2,1)}, u32[]{:S(2)}, u32[]{:S(2)}) collective-permute-start(bf16[512,1024]{0,1:T(8,128)(2,1)} %collective-permute-done.3), channel_id=1, source_target_pairs={{0,2},{2,4},{4,6},{6,8},{8,10},{10,12},{12,14},{14,16},{16,18},{18... | collective-permute-start | bytes 3145736 | tf_op jit(solution)/shard_map/ppermute | solution.py:15
  121.8 39.4 %copy-start = (f32[8,256,256,3]{2,1,3,0:T(8,128)}, f32[8,256,256,3]{2,1,3,0:T(8,128)S(1)}, u32[]{:S(2)}) copy-start(f32[8,256,256,3]{2,1,3,0:T(8,128)S(1)} %get-tuple-element.2461) | copy-start | bytes 18874372
  121.8 42.3 %copy-start.5 = (bf16[256,1024]{1,0:T(8,128)(2,1)S(1)}, bf16[256,1024]{1,0:T(8,128)(2,1)}, u32[]{:S(2)}) copy-start(bf16[256,1024]{1,0:T(8,128)(2,1)} %param.26) | copy-start | bytes 1572868
  133.0 111.7 %collective-permute-start.6 = (bf16[512,1024]{0,1:T(8,128)(2,1)}, bf16[512,1024]{0,1:T(8,128)(2,1)}, u32[]{:S(2)}, u32[]{:S(2)}) collective-permute-start(bf16[512,1024]{0,1:T(8,128)(2,1)} %collective-permute-done.4), channel_id=1, source_target_pairs={{0,2},{2,4},{4,6},{6,8},{8,10},{10,12},{12,14},{14,16},{16,18},{18... | collective-permute-start | bytes 3145736 | tf_op jit(solution)/shard_map/ppermute | solution.py:15
  155.5 89.2 %collective-permute-start.7 = (bf16[512,1024]{0,1:T(8,128)(2,1)}, bf16[512,1024]{0,1:T(8,128)(2,1)}, u32[]{:S(2)}, u32[]{:S(2)}) collective-permute-start(bf16[512,1024]{0,1:T(8,128)(2,1)} %collective-permute-done.5), channel_id=1, source_target_pairs={{0,2},{2,4},{4,6},{6,8},{8,10},{10,12},{12,14},{14,16},{16,18},{18... | collective-permute-start | bytes 3145736 | tf_op jit(solution)/shard_map/ppermute | solution.py:15
Sparse Core Ops, SparseCore 0:
  9.1 16.5 all-gather.1
